TPU v7x, 128 devices: a whole 4x4x4 slice. The times are simulated.
128 devices in a mesh: shard: 32 (over y, z_hi, x), tensor: 4 (over z_lo, core).
Axes of the slice: x: 4, y: 4, z: 4 (z_hi: 2, z_lo: 2; z = z_hi * 2 + z_lo), core: 2. Of those that a mesh axis runs over, the one named last changes fastest.
Arguments:
- acts: bfloat16 [32768, 768], P('shard', 'tensor')
- out_grads: bfloat16 [2, 32768, 768], P(None, 'shard', 'tensor')
- sampled_rows: int32 [2, 262144], P(None, 'shard'), may hold values from 0 to 1023
- proj_grad: float32 [768, 768], P(('shard', 'tensor')), may hold values from -600 to 600
- proj_momentum: float32 [768, 768], P(('shard', 'tensor')), may hold values from -6 to 6
- embed_grad: float32 [49152, 768], P(('shard', 'tensor')), may hold values from -36 to 36
- embed_momentum: float32 [49152, 768], P(('shard', 'tensor')), may hold values from -6 to 6
- token_counts: int32 [49152], P(('shard', 'tensor')), may hold values from 0 to 99
Outputs:
- proj_momentum_new: float32 [768, 768], P(('shard', 'tensor'))
- embed_momentum_new: float32 [49152, 768], P(('shard', 'tensor'))
Inputs may be any that keep to these rules, and one draw needn't show every extreme that they name: `sampled_rows`: entry j of a row picks token (j // 8192) * 1024 + value, one of the 1024 tokens of its index of shard; repeats are allowed.
All inputs are finite; a program needn't handle non-finite values.
Results may differ from a plain program's by a relative error of at most 0.0003.
Values may be sent and summed in bfloat16 or wider, within the bound.
No kernel may reach another device: no remote copies, remote signals or barrier semaphores. Data moves between devices by JAX's collectives and lax.ppermute only.
A program may use at most 128 MiB of HBM per device.

v0:
```python
import jax
import jax.numpy as jnp
from jax import lax
from jax.sharding import PartitionSpec as P

D = 768
VOCAB = 49152
SAMPLE = 2048
NS_ITERS = 3


momentum_decay = 0.9
damping_root = 0.5
count_scale = 64.0
highest = lax.Precision.HIGHEST


def per_device(
    acts,
    out_grads,
    sampled_rows,
    proj_grad,
    proj_momentum,
    embed_grad,
    embed_momentum,
    token_counts,
):
    n_shard = lax.axis_size("shard")
    n_tensor = lax.axis_size("tensor")
    devices_all = n_shard * n_tensor
    flat_index = lax.axis_index("shard") * n_tensor + lax.axis_index("tensor")
    width = D
    row_count = width // devices_all
    sample_total = SAMPLE * devices_all
    picked = jnp.stack(
        [
            jnp.take(acts, sampled_rows[0], axis=0),
            jnp.take(out_grads[0], sampled_rows[0], axis=0),
            jnp.take(out_grads[1], sampled_rows[1], axis=0),
        ]
    )
    sampled = lax.all_to_all(picked, "tensor", split_axis=1, concat_axis=2, tiled=True)
    trace_part = jnp.sum(jnp.square(sampled.astype(jnp.float32)), axis=(1, 2))
    factor_rows = (
        lax.psum_scatter(
            jnp.einsum("fsd,fse->dfe", sampled, sampled, preferred_element_type=jnp.float32),
            ("shard", "tensor"),
            scatter_dimension=0,
            tiled=True,
        )
        / sample_total
    )
    frob_part = jnp.sum(factor_rows * factor_rows, axis=(0, 2))
    count_part = jnp.sum(token_counts).astype(jnp.float32)
    frob_total, trace_total, count_total = lax.psum(
        (frob_part, trace_part, count_part), ("shard", "tensor")
    )
    traces = trace_total / sample_total
    ratio = jnp.sqrt(traces[0] / traces[1])
    embed_ratio = jnp.sqrt(count_total / count_scale / VOCAB / (traces[2] / width))
    shifts = jnp.stack([damping_root * ratio, damping_root / ratio, damping_root / embed_ratio])
    norm_sq = frob_total + 2.0 * shifts * traces + width * shifts * shifts
    start_scale = 1.0 / jnp.sqrt(norm_sq)
    row_ids = flat_index * row_count + jnp.arange(row_count, dtype=jnp.int32)
    eye_rows = (jnp.arange(width, dtype=jnp.int32)[None, :] == row_ids[:, None]).astype(
        jnp.float32
    )[:, None, :]
    damped = factor_rows + shifts[None, :, None] * eye_rows
    rows_now = (
        2.0 * start_scale[None, :, None] * eye_rows
        - (start_scale * start_scale)[None, :, None] * damped
    )
    for iteration in range(NS_ITERS):
        inverses = lax.all_gather(rows_now, ("shard", "tensor"), axis=0, tiled=True)
        if iteration < NS_ITERS - 1:
            product = jnp.einsum("rfk,kfj->rfj", damped, inverses, precision=highest)
            rows_now = 2.0 * rows_now - jnp.einsum(
                "rfk,kfj->rfj", product, inverses, precision=highest
            )
    g_inverse = inverses[:, 1, :]
    e_inverse = inverses[:, 2, :]
    a_rows = lax.dynamic_slice_in_dim(inverses[:, 0, :], flat_index * row_count, row_count, 0)
    mixed_rows = jnp.dot(proj_grad, g_inverse, precision=highest)
    update = jnp.dot(
        a_rows,
        lax.all_gather(mixed_rows, ("shard", "tensor"), axis=0, tiled=True),
        precision=highest,
    )
    row_scale = token_counts.astype(jnp.float32) / count_scale + damping_root * embed_ratio
    embed_update = jnp.dot(embed_grad, e_inverse, precision=highest) / row_scale[:, None]
    return (momentum_decay * proj_momentum + update, momentum_decay * embed_momentum + embed_update)


def solution(mesh):
    return jax.shard_map(
        per_device,
        mesh=mesh,
        in_specs=(
            P("shard", "tensor"),
            P(None, "shard", "tensor"),
            P(None, "shard"),
            P(("shard", "tensor"), None),
            P(("shard", "tensor"), None),
            P(("shard", "tensor"), None),
            P(("shard", "tensor"), None),
            P(("shard", "tensor")),
        ),
        out_specs=(P(("shard", "tensor"), None), P(("shard", "tensor"), None)),
        check_vma=False,
    )
```

profile of v0, /device:TPU:1, one launch (start us, length us, event | category | flops | bytes accessed | tf_op | source)
XLA Modules:
  0.0 1483.3 jit_solution(11976387362760375360)
XLA Ops:
  7.2 1.0 fusion.62
  8.3 1.2 copy.48
  9.5 1.2 fusion.61
  10.7 0.2 copy.72
  10.9 0.2 copy.73
  11.1 32.9 %gather_fusion.1 = bf16[8192,192]{1,0:T(8,128)(2,1)} fusion(bf16[1024,192]{1,0:T(8,128)(2,1)S(1)} %bitcast.65, s32[8192]{0:T(1024)S(1)} %fusion.50), kind=kCustom, calls=%fused_computation.1.clone | custom fusion | bytes 6324224 | tf_op jit(solution)/shard_map/jit(_take)/gather | solution.py:38
  44.0 32.9 %gather_fusion = bf16[8192,192]{1,0:T(8,128)(2,1)} fusion(bf16[1024,192]{1,0:T(8,128)(2,1)S(1)} %copy.48, s32[8192]{0:T(1024)S(1)} %fusion.50), kind=kCustom, calls=%fused_computation.clone | custom fusion | bytes 6324224 | tf_op jit(solution)/shard_map/jit(_take)/gather | solution.py:37
  76.9 32.9 %gather_fusion.2 = bf16[8192,192]{1,0:T(8,128)(2,1)} fusion(bf16[1024,192]{1,0:T(8,128)(2,1)S(1)} %bitcast.64, s32[8192]{0:T(1024)S(1)} %fusion.51), kind=kCustom, calls=%fused_computation.2.clone | custom fusion | bytes 6324224 | tf_op jit(solution)/shard_map/jit(_take)/gather | solution.py:39
  109.9 6.8 select_bitcast_fusion
  116.7 4.3 select_bitcast_fusion.2
  121.0 6.2 pad_maximum_fusion
  127.2 17.9 %copy.51 = bf16[3,8192,192]{2,0,1:T(4,128)(2,1)S(1)} copy(bf16[3,8192,192]{2,1,0:T(8,128)(2,1)} %pad_maximum_fusion) | data formatting | bytes 18874368 | tf_op jit(solution)/shard_map/stack | solution.py:35
  145.1 187.7 %all_to_all.18 = bf16[3,8192,192]{2,0,1:T(4,128)(2,1)} all-to-all(bf16[3,8192,192]{2,0,1:T(4,128)(2,1)S(1)} %copy.51), channel_id=1, replica_groups=mesh['shard'=32,'tensor'=4] {'tensor'}, dimensions={1} | all-to-all | bytes 18874368 | tf_op jit(solution)/shard_map/all_to_all | solution.py:42
  332.8 24.3 %copy.53 = bf16[3,2048,4,192]{1,3,2,0:T(8,128)(2,1)} copy(bf16[3,2048,4,192]{3,0,1,2:T(4,128)(2,1)} %bitcast.66) | data formatting | bytes 18874368 | tf_op jit(solution)/shard_map/all_to_all | solution.py:42
  357.0 14.6 convolution_bitcast_fusion
  371.7 11.0 copy.55
  382.7 0.5 all-gather.6.cloned.1.call-start
  383.2 0.1 copy-done.3
  383.4 0.6 reduce_sum.29
  384.7 26.6 %copy.67 = bf16[3,4,2048,192]{2,1,3,0:T(4,128)(2,1)} copy(bf16[3,4,2048,192]{3,0,2,1:T(4,128)(2,1)} %bitcast.67) | data formatting | bytes 18874368 | tf_op jit(solution)/shard_map/all_to_all | solution.py:42
  411.2 10.6 multiply_reduce_fusion
  421.8 127.8 %all-reduce.4.cloned.1.call-done = f32[768,3,768]{2,1,0:T(4,128)} async-done(((f32[768,3,768]{2,1,0:T(4,128)}), f32[768,3,768]{2,1,0:T(4,128)}) %all-reduce.4.cloned.1.call-update) | async-done | bytes 7077904
  549.6 0.9 constant_dynamic-slice_fusion
  550.5 0.1 multiply_reduce_fusion.1
  550.7 64.2 %all-reduce.1 = (f32[]{:T(128)}, f32[3]{0:T(128)S(1)}, f32[3]{0:T(128)S(1)}) all-reduce(f32[]{:T(128)S(6)} %convert_element_type.18, f32[3]{0:T(128)S(1)} %multiply_reduce_fusion, f32[3]{0:T(128)S(1)} %multiply_reduce_fusion.1), channel_id=1, replica_groups=mesh['shard'=32,'tensor'=4] {'shard','tensor'}, use_global_device_ids=true, to_apply=%region_6.8 | all-reduce | flops 7 | bytes 56 | tf_op jit(solution)/shard_map/psum | solution.py:55
  614.9 0.6 fusion.63
  618.5 0.7 copy.57
  619.2 0.2 all-gather.8.cloned.1.call-start
  619.4 199.9 %all-gather.6.cloned.1.call-done = f32[768,3,768]{2,1,0:T(4,128)} async-done(((f32[6,3,768]{2,1,0:T(4,128)}), f32[768,3,768]{2,1,0:T(4,128)}) %all-gather.6.cloned.1.call-update) | async-done | bytes 7077904 | tf_op jit(solution)/shard_map/all_gather | solution.py:74
  819.3 7.9 fusion.29
  827.2 7.9 fusion.26
  835.1 0.7 copy.60
  835.8 0.3 all-gather.10.cloned.1.call-start
  836.1 201.5 %all-gather.8.cloned.1.call-done = f32[768,3,768]{2,1,0:T(4,128)} async-done(((f32[6,3,768]{2,1,0:T(4,128)}), f32[768,3,768]{2,1,0:T(4,128)}) %all-gather.8.cloned.1.call-update) | async-done | bytes 7077904 | tf_op jit(solution)/shard_map/all_gather | solution.py:74
  1037.6 7.9 fusion.38
  1045.5 7.9 fusion.35
  1053.4 0.7 copy.63
  1054.1 0.3 all-gather.12.cloned.1.call-start
  1054.4 201.6 %all-gather.10.cloned.1.call-done = f32[768,3,768]{2,1,0:T(4,128)} async-done(((f32[6,3,768]{2,1,0:T(4,128)}), f32[768,3,768]{2,1,0:T(4,128)}) %all-gather.10.cloned.1.call-update) | async-done | bytes 7077904 | tf_op jit(solution)/shard_map/all_gather | solution.py:74
  1256.0 16.8 %fusion.60 = (f32[768,1,768]{2,1,0:T(1,128)}, f32[768,1,768]{2,1,0:T(1,128)S(1)}, f32[768,1,768]{2,1,0:T(1,128)S(1)}) fusion(f32[768,3,768]{2,1,0:T(4,128)} %all-gather.10.cloned.1.call-done), kind=kLoop, calls=%fused_computation.66 | loop fusion | bytes 14155776 | tf_op jit(solution)/shard_map/slice | solution.py:81
  1272.8 2.7 fusion.41
  1275.5 2.7 copy.64
  1278.2 10.5 fusion.20
  1288.7 2.7 copy.65
  1291.3 0.6 constant_dynamic-slice_fusion.1
  1291.9 179.2 %all-gather.12.cloned.1.call-done = f32[128,6,768]{2,1,0:T(8,128)} async-done(((f32[1,6,768]{2,1,0:T(8,128)}), f32[128,6,768]{2,1,0:T(8,128)}) %all-gather.12.cloned.1.call-update) | async-done | bytes 2359312 | tf_op jit(solution)/shard_map/all_gather | solution.py:86
  1471.1 2.7 reshape.75
  1473.8 2.6 convolution_add_fusion
  (24 shorter events, 0.5 us)
Async XLA Ops:
  7.2 1271.0 %copy-start = (f32[384,768]{1,0:T(8,128)S(1)}, f32[384,768]{1,0:T(8,128)}, u32[]{:S(2)}) copy-start(f32[384,768]{1,0:T(8,128)} %param.15) | copy-start | bytes 3538948
  7.2 542.4 %all-reduce.4.cloned.1.call-start = ((), (), s32[]{:S(2)}) async-start(), calls=%async_computation.5 | async-start | bytes 18874368
  109.9 6.8 copy-start.1
  109.9 6.9 copy-start.2
  382.7 0.7 copy-start.3
  382.7 436.6 %all-gather.6.cloned.1.call-start = ((), (), s32[]{:S(2)}) async-start(), calls=%async_computation.1 | async-start | bytes 9510912 | tf_op jit(solution)/shard_map/all_gather | solution.py:74
  619.2 418.4 %all-gather.8.cloned.1.call-start = ((), (), s32[]{:S(2)}) async-start(), calls=%async_computation.2 | async-start | bytes 9510912 | tf_op jit(solution)/shard_map/all_gather | solution.py:74
  835.8 420.2 %all-gather.10.cloned.1.call-start = ((), (), s32[]{:S(2)}) async-start(), calls=%async_computation.3 | async-start | bytes 9510912 | tf_op jit(solution)/shard_map/all_gather | solution.py:74
  1054.1 417.0 %all-gather.12.cloned.1.call-start = ((), (), s32[]{:S(2)}) async-start(), calls=%async_computation.4 | async-start | bytes 3170304 | tf_op jit(solution)/shard_map/all_gather | solution.py:86
Sparse Core Ops, SparseCore 0:
  382.8 166.7 all-reduce.3
  619.3 199.9 all-gather.5
  835.9 201.5 all-gather.7
  1054.2 201.7 all-gather.9
  1275.6 195.4 all-gather.11
where the time goes:
time: 1490 us; the launch traced here: 1480 us
  waiting for transfers between devices  910 us (61%)
  blocking collectives  252 us (17%)
  local copies, waits for them, and re-layouts  211 us (14%)
  matrix products  62.1 us (4%)
  other arithmetic  29 us (2%)
  between operations  17.8 us (1%)
    all_gather x3, waiting for transfers between devices, per_device(): inverses = lax.all_gather(rows_now, ('shard', 'tensor'), axis=0, tiled=True)  603 us
    all_to_all x1, blocking collectives, per_device(): lax.all_to_all(picked, 'tensor', split_axis=1, concat_axis=2, tiled=True)  188 us
    all_gather x1, waiting for transfers between devices, per_device(): lax.all_gather(mixed_rows, ('shard', 'tensor'), axis=0, tiled=True)  179 us
    unnamed x6, waiting for transfers between devices  128 us
    psum x1, blocking collectives, per_device(): lax.psum((frob_part, trace_part, count_part), ('shard', 'tensor'))  64.2 us
    all_to_all x2, local copies, waits for them, and re-layouts, per_device(): lax.all_to_all(picked, 'tensor', split_axis=1, concat_axis=2, tiled=True)  50.8 us
    gather x1, local copies, waits for them, and re-layouts, per_device(): jnp.take(out_grads[0], sampled_rows[0], axis=0)  32.9 us
    gather x1, local copies, waits for them, and re-layouts, per_device(): jnp.take(out_grads[1], sampled_rows[1], axis=0)  32.9 us
  transfers between devices with their start and end apart: 5, of which 5 were waited for; matrix products, arithmetic and copies ran while one was open for 4% of the time, Pallas kernels for 0%

commit v1 on v0

v1 whole, which is shorter than its diff:
```python
import jax
import jax.numpy as jnp
from jax import lax
from jax.experimental import pallas as pl
from jax.experimental.pallas import tpu as pltpu
from jax.sharding import Mesh, PartitionSpec as P

D = 768
VOCAB = 49152
SAMPLES = 262144
TERMS = 8
BLK = 128
NB = D // BLK
momentum_decay = 0.9
damping_root = 0.5
count_scale = 64.0
f32 = jnp.float32
bf16 = jnp.bfloat16
CHIPS = ("y", "zhi", "x", "zlo")
G_ROWS = 36
F_ROWS = 64
ROWS = F_ROWS + 2 * G_ROWS + 8

PAIRS = [(i, i) for i in range(NB)] + [(i, j) for i in range(NB) for j in range(i + 1, NB)]
PER = len(PAIRS)
VMEM = pl.BlockSpec(memory_space=pltpu.VMEM)
SMEM = pl.BlockSpec(memory_space=pltpu.SMEM)


def pieces(v, n):
    out = []
    for _ in range(n):
        p = v.astype(bf16)
        out.append(p)
        v = v - p.astype(f32)
    return out


def factor_kernel(meta, samples, x, out):
    core = meta[0]
    first = meta[1]
    tokens = x.shape[1]
    token_ids = lax.broadcasted_iota(jnp.int32, (tokens, BLK), 0) + first
    counts = []
    for k in range(2):

        def count(step, acc):
            row = samples[k : k + 1, pl.ds(pl.multiple_of(step * BLK, BLK), BLK)]
            return acc + jnp.where(token_ids == row, 1.0, 0.0)

        acc = lax.fori_loop(0, samples.shape[1] // BLK, count, jnp.zeros((tokens, BLK), f32), unroll=4)
        counts.append(jnp.sum(acc, axis=1, keepdims=True))
    for m in range(3):
        xs = x[m]
        hi, lo = pieces(xs.astype(f32) * counts[m // 2], 2)
        left = jnp.concatenate([hi, lo], axis=0)
        right = jnp.concatenate([xs, xs], axis=0)
        for i in range(NB):
            block_row = lax.dot_general(
                left[:, i * BLK : (i + 1) * BLK],
                right[:, i * BLK :],
                (((0,), (0,)), ((), ())),
                preferred_element_type=f32,
            ) * (1.0 / SAMPLES)
            for j in range(i, NB):
                b = m * PER + PAIRS.index((i, j))
                block = block_row[:, (j - i) * BLK : (j - i + 1) * BLK].astype(bf16)
                for half in range(2):
                    h = 2 * b + half
                    out[(h // 64 + core) % 2, h % 64] = block[half * 64 : (half + 1) * 64]
    for h in (126, 127):
        out[(h // 64 + core) % 2, h % 64] = jnp.zeros((64, BLK), bf16)


def pack_kernel(meta, parts, grad, counts, out):
    h = meta[0]
    total = jnp.sum(parts[...].astype(f32), axis=0)
    rows = lax.broadcasted_iota(jnp.int32, (64, BLK), 0) + (h % 2) * 64
    lanes = lax.broadcasted_iota(jnp.int32, (64, BLK), 1)
    is_diag = (h // 2) % PER < NB

    def full_sum(v):
        return jnp.sum(jnp.sum(v, axis=1, keepdims=True), axis=0, keepdims=True)

    norm = full_sum(total * total) * jnp.where(is_diag, 1.0, 2.0)
    trace = full_sum(jnp.where((rows == lanes) & is_diag, total, 0.0))
    count = full_sum(counts[...].astype(f32))
    scalars = pieces(norm, 3) + pieces(trace, 3) + pieces(count, 2)
    row8 = lax.broadcasted_iota(jnp.int32, (8, BLK), 0)
    tail = jnp.zeros((8, BLK), f32)
    for r, s in enumerate(scalars):
        tail = jnp.where(row8 == r, s.astype(f32), tail)
    g_hi, g_lo = pieces(grad[...], 2)
    payload = jnp.concatenate(
        [total.astype(bf16).astype(f32), g_hi.astype(f32), g_lo.astype(f32), tail], axis=0
    ).astype(bf16)
    out[...] = jnp.broadcast_to(payload[None], out.shape)


def apply_rows(v, factor, keep, scale, n):
    rows = v.shape[0]
    w = v
    for _ in range(TERMS - 1):
        stacked = jnp.concatenate(pieces(w, n), axis=0)
        product = jnp.dot(stacked, factor[...], preferred_element_type=f32)
        total = product[:rows]
        for p in range(1, n):
            total = total + product[p * rows : (p + 1) * rows]
        w = v + keep * w - scale * total
    return w


def update_kernel(meta, mine, theirs, g_hi, g_lo, embed, embed_mom, counts, proj_mom, out_proj, out_embed, every, factors):
    core = meta[0]
    first_row = meta[1]
    every[core] = mine[...]
    every[1 - core] = theirs[...]
    norms, traces, count_total = [], [], jnp.zeros((1, 1), f32)
    for m in range(3):
        acc = jnp.zeros((16, BLK), f32)
        for h in range(42 * m, 42 * m + 42 + (2 if m == 2 else 0)):
            acc = acc + every[h // 64, h % 64, ROWS - 16 : ROWS, :].astype(f32)
        acc = acc[8:, 0:1]
        norms.append(acc[0:1] + acc[1:2] + acc[2:3])
        traces.append(acc[3:4] + acc[4:5] + acc[5:6])
        count_total = count_total + acc[6:7] + acc[7:8]
    ratio = jnp.sqrt(traces[0] / traces[1])
    embed_ratio = jnp.sqrt(count_total / count_scale / VOCAB / (traces[2] / D))
    shifts = [damping_root * ratio, damping_root / ratio, damping_root / embed_ratio]
    scales = [
        1.0 / jnp.sqrt(norms[m] + 2.0 * shifts[m] * traces[m] + D * shifts[m] * shifts[m])
        for m in range(3)
    ]
    keeps = [1.0 - scales[m] * shifts[m] for m in range(3)]
    for m in range(3):
        for p, (i, j) in enumerate(PAIRS):
            h = 2 * (m * PER + p)
            block = jnp.concatenate(
                [every[h // 64, h % 64, :F_ROWS, :], every[h // 64, (h + 1) % 64, :F_ROWS, :]], axis=0
            )
            factors[m, i * BLK : (i + 1) * BLK, j * BLK : (j + 1) * BLK] = block
            if i != j:
                factors[m, j * BLK : (j + 1) * BLK, i * BLK : (i + 1) * BLK] = block.T
    rows = lax.broadcasted_iota(jnp.int32, (8, D), 0) + first_row
    eye_rows = jnp.where(lax.broadcasted_iota(jnp.int32, (8, D), 1) == rows, 1.0, 0.0)
    left = apply_rows(eye_rows, factors.at[0], keeps[0], scales[0], 3) * scales[0]
    split = pieces(left, 3)
    big = jnp.dot(jnp.concatenate(split, axis=0), g_hi[...], preferred_element_type=f32)
    small = jnp.dot(jnp.concatenate(split[:2], axis=0), g_lo[...], preferred_element_type=f32)
    mixed = big[:8] + big[8:16] + big[16:] + small[:8] + small[8:]
    update = apply_rows(mixed, factors.at[1], keeps[1], scales[1], 3) * scales[1]
    out_proj[...] = momentum_decay * proj_mom[...] + update[:6]
    result = apply_rows(embed[...], factors.at[2], keeps[2], scales[2], 2) * scales[2]
    row_scale = counts[...].astype(f32) / count_scale + damping_root * embed_ratio
    out_embed[...] = momentum_decay * embed_mom[...] + result / row_scale


def per_device(acts, out_grads, sampled_rows, proj_grad, proj_momentum, embed_grad, embed_momentum, token_counts):
    core = lax.axis_index("core")
    chip = lax.axis_index(CHIPS)
    tensor = lax.axis_index(("zlo", "core"))
    tokens = acts.shape[0] // 4
    params = pltpu.CompilerParams(vmem_limit_bytes=56 * 1024 * 1024)
    flat = jnp.stack([acts, out_grads[0], out_grads[1]])
    x = lax.all_to_all(flat, ("zlo", "core"), split_axis=1, concat_axis=2, tiled=True)
    halves = pl.pallas_call(
        factor_kernel,
        out_shape=jax.ShapeDtypeStruct((2, 64, 64, BLK), bf16),
        in_specs=[SMEM, VMEM, VMEM],
        out_specs=VMEM,
        compiler_params=params,
        name="factor",
    )(jnp.stack([core, tensor * tokens]).astype(jnp.int32), sampled_rows, x)
    swap = [(0, 1), (1, 0)]
    pair = halves[0].astype(f32) + lax.ppermute(halves[1], "core", swap).astype(f32)
    parts = lax.all_to_all(pair.astype(bf16), CHIPS, split_axis=0, concat_axis=0, tiled=True)
    payload = pl.pallas_call(
        pack_kernel,
        out_shape=jax.ShapeDtypeStruct((64, ROWS, BLK), bf16),
        in_specs=[SMEM, VMEM, VMEM, VMEM],
        out_specs=VMEM,
        compiler_params=params,
        name="pack",
    )(
        (core * 64 + chip)[None].astype(jnp.int32),
        parts,
        proj_grad.reshape(G_ROWS, BLK),
        token_counts.reshape(3, BLK),
    )
    mine = lax.all_to_all(payload, CHIPS, split_axis=0, concat_axis=0, tiled=True)
    theirs = lax.ppermute(mine, "core", swap)
    g_mine = mine[:, F_ROWS : F_ROWS + 2 * G_ROWS]
    g_theirs = theirs[:, F_ROWS : F_ROWS + 2 * G_ROWS]
    even = jnp.where(core == 0, g_mine, g_theirs)
    odd = jnp.where(core == 0, g_theirs, g_mine)
    g_all = jnp.stack([even, odd], axis=1)
    g_hi = g_all[:, :, :G_ROWS].reshape(D, D)
    g_lo = g_all[:, :, G_ROWS:].reshape(D, D)
    first_row = (chip * 2 + core) * 6
    return pl.pallas_call(
        update_kernel,
        out_shape=(
            jax.ShapeDtypeStruct(proj_momentum.shape, f32),
            jax.ShapeDtypeStruct(embed_momentum.shape, f32),
        ),
        in_specs=[SMEM] + [VMEM] * 8,
        out_specs=(VMEM, VMEM),
        scratch_shapes=[pltpu.VMEM((2, 64, ROWS, BLK), bf16), pltpu.VMEM((3, D, D), bf16)],
        compiler_params=params,
        name="update",
    )(
        jnp.stack([core, first_row]).astype(jnp.int32),
        mine,
        theirs,
        g_hi,
        g_lo,
        embed_grad,
        embed_momentum,
        token_counts[:, None],
        proj_momentum,
    )


def solution(mesh):
    fine = Mesh(mesh.devices.reshape(4, 2, 4, 2, 2), ("y", "zhi", "x", "zlo", "core"))
    shard = ("y", "zhi", "x")
    tensor = ("zlo", "core")
    rows = P(shard + tensor, None)
    return jax.shard_map(
        per_device,
        mesh=fine,
        in_specs=(
            P(shard, tensor),
            P(None, shard, tensor),
            P(None, shard),
            rows,
            rows,
            rows,
            rows,
            P(shard + tensor),
        ),
        out_specs=(rows, rows),
        check_vma=False,
    )
```

time: 1490 us -> 148 us (0.10)
  waiting for transfers between devices: 910 us -> 46.6 us
  blocking collectives: 252 us -> 36.1 us
  local copies, waits for them, and re-layouts: 211 us -> 13.3 us
  matrix products: 62.1 us -> 0 us
  Pallas kernels: 0 us -> 25.3 us
  other arithmetic: 29 us -> 5.91 us
  starting transfers between devices: 1.31 us -> 20 us
  between operations: 17.8 us -> 0.71 us
    all_gather x4 -> x0, waiting for transfers between devices: 782 us -> none  [the longest x3 603 us: per_device(): inverses = lax.all_gather(rows_now, ('shard', 'tensor'), axis=0, tiled=True)]
    all_to_all x1, blocking collectives: 188 us -> 36.1 us  [per_device(): lax.all_to_all(payload, CHIPS, split_axis=0, concat_axis=0, tiled=True)]
    unnamed x6 -> x0, waiting for transfers between devices: 128 us -> none
    gather x3 -> x0, local copies, waits for them, and re-layouts: 98.7 us -> none  [the longest x1 32.9 us: per_device(): jnp.take(out_grads[0], sampled_rows[0], axis=0)]
    psum x1 -> x0, blocking collectives: 64.2 us -> none  [per_device(): lax.psum((frob_part, trace_part, count_part), ('shard', 'tensor'))]
    dot_general x8 -> x0, matrix products: 62.1 us -> none  [the longest x2 15.9 us: per_device(): product = jnp.einsum('rfk,kfj->rfj', damped, inverses, precision=highest)]
    all_to_all x2, local copies, waits for them, and re-layouts: 50.8 us -> 2.69 us  [per_device(): lax.all_to_all(flat, ('zlo', 'core'), split_axis=1, concat_axis=2, tiled=...]
    all_to_all x0 -> x2, waiting for transfers between devices: none -> 41.4 us  [the longest x1 24.1 us: per_device(): lax.all_to_all(flat, ('zlo', 'core'), split_axis=1, concat_axis=2, tiled=...]
  transfers between devices with their start and end apart: 5 -> 4, of which waited for: 5 -> 4; matrix products, arithmetic and copies ran while one was open for 4% -> 2% of each run, Pallas kernels for 0% -> 0%
where the time goes in v1:
time: 148 us
  waiting for transfers between devices  46.6 us (31%)
  blocking collectives  36.1 us (24%)
  Pallas kernels  25.3 us (17%)
  starting transfers between devices  20 us (14%)
  local copies, waits for them, and re-layouts  13.3 us (9%)
  other arithmetic  5.91 us (4%)
    all_to_all x1, blocking collectives, per_device(): lax.all_to_all(payload, CHIPS, split_axis=0, concat_axis=0, tiled=True)  36.1 us
    all_to_all x1, waiting for transfers between devices, per_device(): lax.all_to_all(flat, ('zlo', 'core'), split_axis=1, concat_axis=2, tiled=...  24.1 us
    all_to_all x1, waiting for transfers between devices, per_device(): lax.all_to_all(pair.astype(bf16), CHIPS, split_axis=0, concat_axis=0, til...  17.3 us
    pallas_call x1, Pallas kernels, per_device(): pl.pallas_call(update_kernel, out_shape=(jax.ShapeDtypeStruct(proj_moment...  15.9 us
    all_to_all x1, starting transfers between devices, per_device(): lax.all_to_all(pair.astype(bf16), CHIPS, split_axis=0, concat_axis=0, til...  11.2 us
    pallas_call x1, Pallas kernels, per_device(): pl.pallas_call(factor_kernel, out_shape=jax.ShapeDtypeStruct((2, 64, 64,...  6.39 us
    all_to_all x1, starting transfers between devices, per_device(): lax.all_to_all(flat, ('zlo', 'core'), split_axis=1, concat_axis=2, tiled=...  4.95 us
    pallas_call x1, Pallas kernels, per_device(): pl.pallas_call(pack_kernel, out_shape=jax.ShapeDtypeStruct((64, ROWS, BLK...  3 us
  transfers between devices with their start and end apart: 4, of which 4 were waited for; matrix products, arithmetic and copies ran while one was open for 2% of the time, Pallas kernels for 0%

profile of v1, /device:TPU:1, one launch (start us, length us, event | category | flops | bytes accessed | tf_op | source)
XLA Modules:
  0.0 147.9 jit_solution(16893368940120597138)
XLA Ops:
  0.6 1.3 pad_maximum_fusion.1
  2.0 2.5 %copy.38 = bf16[3,1024,192]{2,0,1:T(4,128)(2,1)} copy(bf16[3,1024,192]{1,2,0:T(8,128)(2,1)S(1)} %pad_maximum_fusion.1) | data formatting | bytes 2359296 | tf_op jit(solution)/shard_map/stack | solution.py:164
  4.5 5.0 %all-to-all-start = ((bf16[3,1024,192]{2,0,1:T(4,128)(2,1)}), bf16[3,1024,192]{2,0,1:T(4,128)(2,1)S(1)}, u32[]{:S(2)}, u32[]{:S(2)}) async-start(bf16[3,1024,192]{2,0,1:T(4,128)(2,1)} %copy.38), calls=%async_computation | async-start | bytes 4194304 | tf_op jit(solution)/shard_map/all_to_all | solution.py:165
  9.5 0.6 pad_add_fusion.1.meta
  10.0 24.1 %all-to-all-done = bf16[3,1024,192]{2,0,1:T(4,128)(2,1)S(1)} async-done(((bf16[3,1024,192]{2,0,1:T(4,128)(2,1)}), bf16[3,1024,192]{2,0,1:T(4,128)(2,1)S(1)}, u32[]{:S(2)}, u32[]{:S(2)}) %all-to-all-start) | async-done | bytes 1179680 | tf_op jit(solution)/shard_map/all_to_all | solution.py:165
  34.2 1.2 copy.40
  35.3 1.5 %copy.41.x = bf16[3,256,768]{2,1,0:T(8,128)(2,1)} copy(bf16[3,256,768]{1,2,0:T(8,128)(2,1)S(1)} %bitcast.23) | data formatting | bytes 2359296 | tf_op jit(solution)/shard_map/all_to_all | solution.py:165
  36.8 6.4 %factor.1 = bf16[2,64,64,128]{3,2,1,0:T(8,128)(2,1)} custom-call(s32[2]{0:T(128)} %pad_add_fusion.1.meta, s32[2,8192]{1,0:T(2,128)} %samples.1, bf16[3,256,768]{2,1,0:T(8,128)(2,1)} %copy.41.x), custom_call_target="tpu_custom_call" | custom-call | tf_op jit(solution)/shard_map/factor/pallas_call | solution.py:166
  43.2 0.0 copy-start.1
  43.2 1.4 slice_bitcast_fusion
  44.7 1.1 collective-permute-start
  45.7 2.3 %collective-permute-done = bf16[64,64,128]{2,1,0:T(8,128)(2,1)S(1)} collective-permute-done((bf16[64,64,128]{2,1,0:T(8,128)(2,1)S(1)}, bf16[64,64,128]{2,1,0:T(8,128)(2,1)S(1)}, u32[]{:S(2)}, u32[]{:S(2)}) %collective-permute-start) | collective-permute-done | bytes 1048608 | tf_op jit(solution)/shard_map/ppermute | solution.py:175
  48.0 0.0 copy-done.1
  48.0 1.4 fusion
  49.4 0.0 copy-start.3
  49.4 11.2 %all-to-all-start.1 = ((bf16[64,64,128]{2,1,0:T(8,128)(2,1)}), bf16[64,64,128]{2,1,0:T(8,128)(2,1)S(1)}, u32[]{:S(2)}, u32[]{:S(2)}) async-start(bf16[64,64,128]{2,1,0:T(8,128)(2,1)} %fusion), calls=%async_computation.1 | async-start | bytes 2097152 | tf_op jit(solution)/shard_map/all_to_all | solution.py:176
  60.6 0.0 copy-done.3
  60.7 0.6 reshape.18.grad
  61.3 17.3 %all-to-all-done.1.parts = bf16[64,64,128]{2,1,0:T(8,128)(2,1)S(1)} async-done(((bf16[64,64,128]{2,1,0:T(8,128)(2,1)}), bf16[64,64,128]{2,1,0:T(8,128)(2,1)S(1)}, u32[]{:S(2)}, u32[]{:S(2)}) %all-to-all-start.1) | async-done | bytes 1048608 | tf_op jit(solution)/shard_map/all_to_all | solution.py:176
  78.6 0.0 copy-start.2
  78.6 1.0 copy-done.2
  79.5 3.0 %pack.1 = bf16[64,144,128]{2,1,0:T(8,128)(2,1)} custom-call(s32[1]{0:T(128)} %bitcast.2.meta, bf16[64,64,128]{2,1,0:T(8,128)(2,1)} %copy-done.2, f32[36,128]{1,0:T(8,128)} %reshape.18.grad, s32[3,128]{1,0:T(4,128)} %bitcast.25), custom_call_target="tpu_custom_call" | custom-call | tf_op jit(solution)/shard_map/pack/pallas_call | solution.py:177
  82.5 0.0 copy-start.4
  82.5 36.1 %all_to_all.28.mine = bf16[64,144,128]{2,1,0:T(8,128)(2,1)S(1)} all-to-all(bf16[64,144,128]{2,1,0:T(8,128)(2,1)} %pack.1), channel_id=1, replica_groups=mesh['y'=4,'zhi'=2,'x'=4,'zlo'=2,'core'=2] {'y','zhi','x','zlo'}, dimensions={0} | all-to-all | bytes 4718592 | tf_op jit(solution)/shard_map/all_to_all | solution.py:190
  118.7 0.0 copy-start
  118.7 2.7 %collective-permute-start.1 = (bf16[64,144,128]{2,1,0:T(8,128)(2,1)S(1)}, bf16[64,144,128]{2,1,0:T(8,128)(2,1)}, u32[]{:S(2)}, u32[]{:S(2)}) collective-permute-start(bf16[64,144,128]{2,1,0:T(8,128)(2,1)S(1)} %all_to_all.28.mine), channel_id=1, source_target_pairs={{0,1},{1,0},{2,3},{3,2},{4,5},{5,4},{6,7},{7,6},{8,9},{9,8},{10,11... | collective-permute-start | bytes 7077896 | tf_op jit(solution)/shard_map/ppermute | solution.py:191
  121.4 0.0 copy-done.4
  121.4 0.8 broadcast_in_dim.8.counts
  122.2 0.6 pad_add_fusion.meta
  122.8 2.9 %collective-permute-done.1.theirs = bf16[64,144,128]{2,1,0:T(8,128)(2,1)} collective-permute-done((bf16[64,144,128]{2,1,0:T(8,128)(2,1)S(1)}, bf16[64,144,128]{2,1,0:T(8,128)(2,1)}, u32[]{:S(2)}, u32[]{:S(2)}) %collective-permute-start.1) | collective-permute-done | bytes 2359328 | tf_op jit(solution)/shard_map/ppermute | solution.py:191
  125.7 1.4 select_bitcast_fusion
  127.1 0.0 copy-done
  127.1 0.6 pad_maximum_fusion
  127.8 0.1 copy.42
  127.9 2.0 %reshape.20.g_hi = bf16[768,768]{1,0:T(8,128)(2,1)} reshape(bf16[64,2,36,128]{3,2,1,0:T(8,128)(2,1)S(1)} %copy.42) | data formatting | bytes 2359296 | tf_op jit(solution)/shard_map/reshape | solution.py:197
  129.9 0.1 copy.43
  130.0 2.0 %reshape.21.g_lo = bf16[768,768]{1,0:T(8,128)(2,1)} reshape(bf16[64,2,36,128]{3,2,1,0:T(8,128)(2,1)S(1)} %copy.43) | data formatting | bytes 2359296 | tf_op jit(solution)/shard_map/reshape | solution.py:198
  132.0 15.9 %update.1 = (f32[6,768]{1,0:T(8,128)}, f32[384,768]{1,0:T(8,128)}) custom-call(s32[2]{0:T(128)} %pad_add_fusion.meta, bf16[64,144,128]{2,1,0:T(8,128)(2,1)} %copy-done, bf16[64,144,128]{2,1,0:T(8,128)(2,1)} %collective-permute-done.1.theirs, bf16[768,768]{1,0:T(8,128)(2,1)} %reshape.20.g_hi, bf16[768,768]{1,0:T(8,128)(2,1)} %reshape.21.g_lo, ...), custom_call_target="tpu_custom_call" | custom-call | tf_op jit(solution)/shard_map/update/pallas_call | solution.py:200
Async XLA Ops:
  4.5 29.6 %all-to-all-start = ((bf16[3,1024,192]{2,0,1:T(4,128)(2,1)}), bf16[3,1024,192]{2,0,1:T(4,128)(2,1)S(1)}, u32[]{:S(2)}, u32[]{:S(2)}) async-start(bf16[3,1024,192]{2,0,1:T(4,128)(2,1)} %copy.38), calls=%async_computation | async-start | bytes 4194304 | tf_op jit(solution)/shard_map/all_to_all | solution.py:165
  43.2 4.8 %copy-start.1 = (bf16[2,64,64,128]{3,2,1,0:T(8,128)(2,1)S(1)}, bf16[2,64,64,128]{3,2,1,0:T(8,128)(2,1)}, u32[]{:S(2)}) copy-start(bf16[2,64,64,128]{3,2,1,0:T(8,128)(2,1)} %factor.1) | copy-start | bytes 6291460
  44.7 3.4 %collective-permute-start = (bf16[64,64,128]{2,1,0:T(8,128)(2,1)S(1)}, bf16[64,64,128]{2,1,0:T(8,128)(2,1)S(1)}, u32[]{:S(2)}, u32[]{:S(2)}) collective-permute-start(bf16[64,64,128]{2,1,0:T(8,128)(2,1)S(1)} %slice_bitcast_fusion), channel_id=1, source_target_pairs={{0,1},{1,0},{2,3},{3,2},{4,5},{5,4},{6,7},{7,6},{8,9},{9,8},{10,11... | collective-permute-start | bytes 3145736 | tf_op jit(solution)/shard_map/ppermute | solution.py:175
  49.4 11.2 %copy-start.3 = (f32[6,768]{1,0:T(8,128)S(1)}, f32[6,768]{1,0:T(8,128)}, u32[]{:S(2)}) copy-start(f32[6,768]{1,0:T(8,128)} %param.11) | copy-start | bytes 55300
  49.4 29.2 %all-to-all-start.1 = ((bf16[64,64,128]{2,1,0:T(8,128)(2,1)}), bf16[64,64,128]{2,1,0:T(8,128)(2,1)S(1)}, u32[]{:S(2)}, u32[]{:S(2)}) async-start(bf16[64,64,128]{2,1,0:T(8,128)(2,1)} %fusion), calls=%async_computation.1 | async-start | bytes 2097152 | tf_op jit(solution)/shard_map/all_to_all | solution.py:176
  78.6 1.0 copy-start.2
  82.5 38.8 %copy-start.4 = (s32[384]{0:T(512)S(1)}, s32[384]{0:T(512)}, u32[]{:S(2)}) copy-start(s32[384]{0:T(512)} %param.15) | copy-start | bytes 4612
  118.7 8.5 %copy-start = (bf16[64,144,128]{2,1,0:T(8,128)(2,1)}, bf16[64,144,128]{2,1,0:T(8,128)(2,1)S(1)}, u32[]{:S(2)}) copy-start(bf16[64,144,128]{2,1,0:T(8,128)(2,1)S(1)} %all_to_all.28.mine) | copy-start | bytes 7077892
  118.7 7.0 %collective-permute-start.1 = (bf16[64,144,128]{2,1,0:T(8,128)(2,1)S(1)}, bf16[64,144,128]{2,1,0:T(8,128)(2,1)}, u32[]{:S(2)}, u32[]{:S(2)}) collective-permute-start(bf16[64,144,128]{2,1,0:T(8,128)(2,1)S(1)} %all_to_all.28.mine), channel_id=1, source_target_pairs={{0,1},{1,0},{2,3},{3,2},{4,5},{5,4},{6,7},{7,6},{8,9},{9,8},{10,11... | collective-permute-start | bytes 7077896 | tf_op jit(solution)/shard_map/ppermute | solution.py:191
